TPU v7x, 32 devices: a whole 2x2x4 slice. The times are simulated.
32 devices in a mesh: groups: 2 (over x), dp: 4 (over z), tensor: 4 (over y, core).
Axes of the slice: x: 2, y: 2, z: 4, core: 2. Of those that a mesh axis runs over, the one named last changes fastest.
Arguments:
- patches: float32 [16, 256, 6144], P(('groups', 'dp'), None, 'tensor'), parts along dimension 0, may hold values from -60 to 60
- counts: int32 [16], P(('groups', 'dp')), parts along dimension 0, may hold values from 1 to 63, as said below
- ranking: int32 [16, 256], P(('groups', 'dp')), parts along dimension 0, may hold values from 0 to 255, each once within a row
- norm_gain: float32 [6144], P('tensor'), may hold values from 0.1 to 1.9
- expand_weight: bfloat16 [24576, 6144], P(('dp', 'tensor')), may hold values from -0.078125 to 0.078125
- expand_bias: bfloat16 [24576], P(('dp', 'tensor')), may hold values from -4 to 4
- reduce_weight: bfloat16 [24576, 6144], P(('dp', 'tensor')), may hold values from -0.078125 to 0.078125
- reduce_bias: float32 [6144], P('tensor'), may hold values from -4 to 4
Outputs:
- updated: float32 [16, 256, 6144], P(('groups', 'dp'), None, 'tensor'), parts along dimension 0
There are 2 independent parts, one for each index of `groups`. A program takes and returns all parts, laid end to end along the dimension named above; an argument that names none is the same for every part. Nothing has to cross between parts.
Inputs may be any that keep to these rules, and one draw needn't show every extreme that they name: The counts of the 2 images of one index of dp (images b * 2 to (b + 1) * 2 - 1) sum to at most 64; in every draw one such group sums to exactly 64, and some image holds exactly 63.
All inputs are finite; a program needn't handle non-finite values.
Results may differ from a plain program's by a relative error of at most 0.00061.
Values may be sent and summed in bfloat16 or wider, within the bound.
A program may use at most 128 MiB of HBM per device.

v0:
```python
import functools

import jax
import jax.numpy as jnp
from jax import lax
from jax.experimental import pallas as pl
from jax.experimental.pallas import tpu as pltpu
from jax.sharding import PartitionSpec as P

CAP = 64
MESH = pl.DeviceIdType.MESH


def block_kernel(
    Z, T, C, C2, counts, ranking, ranking_v, gain, ebias, rbias, flat, e_hbm, r_hbm, out,
    pt, rows, pick,    xg, wv, rv, pre, hid, bias, last, st, cs, cr, own, ys, yr, zs, zr,
    psem, osem, wsem, rsem, st_s, st_r, za_s, za_r, ya_s, ya_r, ca_s, ca_r,
    cr_s, cr_r, yr_s, yr_r, zr_s, zr_r,
):
    Y = T // 2
    R, dl = rows.shape
    images, patch_len = ranking.shape
    N = images * patch_len
    hl, D = e_hbm.shape
    M, dlc, w2 = Z * R, dl // C, dl // C2
    nt = 256 if hl % 256 == 0 else hl
    z = lax.axis_index("dp")
    t = lax.axis_index("tensor")
    y, c = t // 2, t % 2
    z_next = lax.rem(z + 1, Z)
    t_next = lax.rem(y + 1, Y) * 2 + c
    t_part = y * 2 + 1 - c

    barrier = pltpu.get_barrier_semaphore()
    for k in range(1, Z):
        pl.semaphore_signal(barrier, inc=1, device_id={"dp": lax.rem(z + k, Z)}, device_id_type=MESH)
    for k in range(1, T):
        pl.semaphore_signal(barrier, inc=1, device_id={"tensor": lax.rem(t + k, T)}, device_id_type=MESH)

    def copy(src, dst, ss, rs, axis, index):
        return pltpu.make_async_remote_copy(
            src_ref=src, dst_ref=dst, send_sem=ss, recv_sem=rs,
            device_id={axis: index}, device_id_type=MESH,
        )

    def t_of(u, core):
        return lax.rem(y - u + Y, Y) * 2 + core

    def t_red(u, core):
        return lax.rem(y - 1 - u + 2 * Y, Y) * 2 + core

    order = []
    for u in range(Y):
        for core in (c, 1 - c):
            for p in range(C):
                order.append((t_of(u, core), p))

    def expand_load(i):
        block, p = order[i]
        lanes = pl.ds(pl.multiple_of(block * dl + p * dlc, 128), dlc)
        return pltpu.make_async_copy(e_hbm.at[:, lanes], wv.at[i], wsem.at[i])

    def reduce_load(i):
        block = t_red(i // 2, c if i % 2 == 0 else 1 - c)
        lanes = pl.ds(pl.multiple_of(block * dl, 128), dl)
        return pltpu.make_async_copy(r_hbm.at[:, lanes], rv.at[i], rsem.at[i])

    patch_load = pltpu.make_async_copy(flat, pt, psem)
    patch_load.start()

    lane_w = images * R
    which = lax.broadcasted_iota(jnp.int32, (1, lane_w), 1)
    rank, owner = jnp.full((1, lane_w), -1, jnp.int32), jnp.full((1, lane_w), -1, jnp.int32)
    start = 0
    for i in range(images):
        k = which - i * R
        live = (k >= 0) & (k < counts[i])
        owner = jnp.where(live, start + k, owner)
        start = start + counts[i]
        known = jnp.concatenate([ranking_v[i : i + 1, :R]] * images, axis=1)
        rank = jnp.where(live, i * patch_len + known, rank)
    chosen = jnp.where(lax.broadcasted_iota(jnp.int32, (N, lane_w), 0) == rank, 1.0, 0.0)
    slot = jnp.where(lax.broadcasted_iota(jnp.int32, (R, lane_w), 0) == owner, 1.0, 0.0)
    pick[...] = lax.dot_general(
        chosen.astype(jnp.bfloat16), slot.astype(jnp.bfloat16), (((1,), (1,)), ((), ())),
        preferred_element_type=jnp.float32,
    ).astype(jnp.bfloat16)

    def take(j, carry):
        start, source = 0, 0
        for i in range(images):
            offset = j - start
            inside = (offset >= 0) & (offset < counts[i])
            here = i * patch_len + ranking[i, jnp.clip(offset, 0, patch_len - 1)]
            source = jnp.where(inside, here, source)
            start = start + counts[i]
        rows[pl.ds(j, 1), :] = pt[pl.ds(source, 1), :]
        return carry

    patch_load.wait()
    for i in range(T * C):
        expand_load(i).start()
    for i in range(T):
        reduce_load(i).start()
    lax.fori_loop(0, R, take, 0, unroll=8)

    bias[...] = ebias[...].astype(jnp.float32)[None, :]
    x = rows[...]
    s1 = jnp.sum(x, axis=1, keepdims=True)
    s2 = jnp.sum(x * x, axis=1, keepdims=True)
    lane = lax.broadcasted_iota(jnp.int32, (R, 128), 1)
    st[t] = jnp.where(lane == 0, s1, s2)
    pl.semaphore_wait(barrier, Z + T - 2)

    def stat_copy(k):
        return copy(st.at[t], st.at[t], st_s.at[k - 1], st_r.at[k - 1], "tensor", lax.rem(t + k, T))

    for k in range(1, T):
        stat_copy(k).start()
    for k in range(1, T):
        stat_copy(k).wait_recv()
    total = st[0]
    for k in range(1, T):
        total = total + st[k]
    gain_row = gain[...][None, :]
    mean = total[:, 0:1] / D
    var = total[:, 1:2] / D - mean * mean
    scale = lax.rsqrt(var + 1e-06)
    mine = pl.ds(pl.multiple_of(z * R, R), R)
    for p in range(C):
        cols = slice(p * dlc, (p + 1) * dlc)
        xg[t, p, mine, :] = ((rows[:, cols] - mean) * scale * gain_row[:, cols]).astype(jnp.bfloat16)

    def block(tt, j, p):
        return xg.at[tt, p, pl.ds(pl.multiple_of(lax.rem(z - j + Z, Z) * R, R), R), :]

    def z_copy(s, p):
        b = block(t, s - 1, p)
        return copy(b, b, za_s.at[s - 1, p], za_r.at[s - 1, p], "dp", z_next)

    def y_copy(u, j, p):
        b = block(t_of(u - 1, c), j, p)
        return copy(b, b, ya_s.at[u - 1, j, p], ya_r.at[u - 1, j, p], "tensor", t_next)

    def c_copy(u, j, p):
        b = block(t_of(u, c), j, p)
        return copy(b, b, ca_s.at[u, j, p], ca_r.at[u, j, p], "tensor", t_part)

    def expand(i):
        tt, p = order[i]
        expand_load(i).wait()

        acc = lax.dot_general(
            wv[i], xg[tt, p], (((1,), (1,)), ((), ())), preferred_element_type=jnp.float32
        )
        pre[...] = acc if i == 0 else pre[...] + acc

    def expand_partner(u, p):
        for j in range(Z):
            c_copy(u, j, p).wait_recv()
        expand((2 * u + 1) * C + p)

    def y_arrived(u, j, p):
        y_copy(u, j, p).wait_recv()
        if u < Y - 1:
            y_copy(u + 1, j, p).start()
        c_copy(u, j, p).start()

    for p in range(C):
        z_copy(1, p).start()
        y_copy(1, 0, p).start()
        c_copy(0, 0, p).start()
    for s in range(1, Z):
        for p in range(C):
            z_copy(s, p).wait_recv()
            if s < Z - 1:
                z_copy(s + 1, p).start()
            y_copy(1, s, p).start()
            c_copy(0, s, p).start()
            if s == Z - 1:
                expand(p)
        for p in range(C):
            y_arrived(1, s - 1, p)
    for p in range(C):
        expand_partner(0, p)
    for u in range(1, Y):
        for j in range(Z - 1 if u == 1 else 0, Z):
            for p in range(C):
                y_arrived(u, j, p)
                if j == Z - 1:
                    expand(2 * u * C + p)
                    if p > 0:
                        expand_partner(u, p - 1)
        expand_partner(u, C - 1)

    def activate(n):
        units = slice(None) if nt == hl else pl.ds(pl.multiple_of(n * nt, nt), nt)
        v = pre[units, :].T + bias[:, units]
        hid[:, units] = jax.nn.gelu(v, approximate=True).astype(jnp.bfloat16)

    if nt == hl:
        activate(0)
    else:
        lax.fori_loop(0, hl // nt, lambda n, a: (activate(n), a)[1], 0)

    def cr_copy(u, p):
        return copy(cs.at[u, p], cr.at[u, p], cr_s.at[u, p], cr_r.at[u, p], "tensor", t_part)

    def yr_copy(u, p, h):
        half = slice(h * M // 2, (h + 1) * M // 2)
        return copy(
            ys.at[u - 1, p, half, :], yr.at[u - 1, p, half, :],
            yr_s.at[u - 1, p, h], yr_r.at[u - 1, p, h], "tensor", t_next,
        )

    def zr_copy(k, p):
        there = lax.rem(z + k, Z)
        part = pl.ds(pl.multiple_of(there * R, R), R)
        return copy(zs.at[p, part, :], zr.at[k - 1, p], zr_s.at[k - 1, p], zr_r.at[k - 1, p], "dp", there)

    def columns(p):
        return slice(None) if C2 == 1 else pl.ds(pl.multiple_of(p * w2, w2), w2)

    def product(i, p):
        return jnp.dot(hid[...], rv[i, :, columns(p)], preferred_element_type=jnp.float32)

    def produce(u, p):
        cs[u, p] = product(2 * u + 1, p).astype(jnp.bfloat16)
        cr_copy(u, p).start()
        own[u, p] = product(2 * u, p)

    def combine(u, p):
        cr_copy(u, p).wait_recv()
        v = own[u, p] + cr[u, p].astype(jnp.float32)
        if u == 0:
            ys[0, p] = v.astype(jnp.bfloat16)
            for h in range(2):
                yr_copy(1, p, h).start()
        else:
            own[u, p] = v

    def loop(low, high, body):
        lax.fori_loop(low, high, lambda p, a: (body(p), a)[1], 0)

    for u in range(Y):
        reduce_load(2 * u).wait()
        reduce_load(2 * u + 1).wait()
        produce(u, 0)
        if u > 0:
            combine(u - 1, C2 - 1)

        def step(p):
            produce(u, p)
            combine(u, p - 1)

        if C2 > 1:
            loop(1, C2, step)
    combine(Y - 1, C2 - 1)

    for u in range(1, Y):

        def pass_on(p):
            for h in range(2):
                yr_copy(u, p, h).wait_recv()
                half = slice(h * M // 2, (h + 1) * M // 2)
                v = own[u, p, half, :] + yr[u - 1, p, half, :].astype(jnp.float32)
                if u < Y - 1:
                    ys[u, p, half, :] = v.astype(jnp.bfloat16)
                    yr_copy(u + 1, p, h).start()
                else:
                    own[u, p, half, :] = v
                    zs[p, half, :] = v.astype(jnp.bfloat16)
                    for there in range(h * Z // 2, (h + 1) * Z // 2):

                        @pl.when(there != z)
                        def _():
                            zr_copy(lax.rem(there - z + Z, Z), p).start()

        loop(0, C2, pass_on)

    last[...] = rbias[...][None, :]

    def finish(p):
        acc = own[Y - 1, p, mine, :]
        for k in range(1, Z):
            zr_copy(k, p).wait_recv()
            acc = acc + zr[k - 1, p].astype(jnp.float32)
        cols = columns(p)
        add = acc + last[:, cols]
        top = add.astype(jnp.bfloat16)
        rest = add - top.astype(jnp.float32)
        middle = rest.astype(jnp.bfloat16)
        low = (rest - middle.astype(jnp.float32)).astype(jnp.bfloat16)
        spread = jnp.dot(pick[...], low, preferred_element_type=jnp.float32)
        spread = spread + jnp.dot(pick[...], middle, preferred_element_type=jnp.float32)
        spread = spread + jnp.dot(pick[...], top, preferred_element_type=jnp.float32)
        pt[:, cols] = pt[:, cols] + spread
        save(p).start()

    def save(p):
        cols = columns(p)
        return pltpu.make_async_copy(pt.at[:, cols], out.at[:, cols], osem.at[p])

    loop(0, C2, finish)

    for k in range(1, T):
        stat_copy(k).wait_send()
    for p in range(C):
        for s in range(1, Z):
            z_copy(s, p).wait_send()
        for j in range(Z):
            for u in range(1, Y):
                y_copy(u, j, p).wait_send()
            for u in range(Y):
                c_copy(u, j, p).wait_send()

    def drain(p):
        save(p).wait()
        for u in range(Y):
            cr_copy(u, p).wait_send()
        for u in range(1, Y):
            for h in range(2):
                yr_copy(u, p, h).wait_send()
        for k in range(1, Z):
            zr_copy(k, p).wait_send()

    loop(0, C2, drain)


def body(
    Z, T, patches, counts, ranking, norm_gain, expand_weight, expand_bias, reduce_weight, reduce_bias
):
    images, patch_len, dl = patches.shape
    hl, D = expand_weight.shape
    flat = patches.reshape(images * patch_len, dl)
    R, M, Y = CAP, Z * CAP, T // 2
    C = 3 if dl % 768 == 0 else 1
    w2 = 512 if dl % 512 == 0 else dl
    C2 = dl // w2
    dlc = dl // C
    vmem = pl.BlockSpec(memory_space=pltpu.VMEM)
    hbm = pl.BlockSpec(memory_space=pl.ANY)
    bf16, f32 = jnp.bfloat16, jnp.float32
    dma = pltpu.SemaphoreType.DMA
    N = images * patch_len
    smem = pl.BlockSpec(memory_space=pltpu.SMEM)
    result = pl.pallas_call(
        functools.partial(block_kernel, Z, T, C, C2),
        out_shape=jax.ShapeDtypeStruct((N, dl), f32),
        in_specs=[smem] * 2 + [vmem] * 4 + [hbm] * 3,
        out_specs=hbm,
        scratch_shapes=[
            pltpu.VMEM((N, dl), f32),
            pltpu.VMEM((R, dl), f32),
            pltpu.VMEM((N, R), bf16),
            pltpu.VMEM((T, C, M, dlc), bf16),
            pltpu.VMEM((T * C, hl, dlc), bf16),
            pltpu.VMEM((T, hl, dl), bf16),
            pltpu.VMEM((hl, M), f32),
            pltpu.VMEM((M, hl), bf16),
            pltpu.VMEM((1, hl), f32),
            pltpu.VMEM((1, dl), f32),
            pltpu.VMEM((T, R, 128), f32),
            pltpu.VMEM((Y, C2, M, w2), bf16),
            pltpu.VMEM((Y, C2, M, w2), bf16),
            pltpu.VMEM((Y, C2, M, w2), f32),
            pltpu.VMEM((Y - 1, C2, M, w2), bf16),
            pltpu.VMEM((Y - 1, C2, M, w2), bf16),
            pltpu.VMEM((C2, M, w2), bf16),
            pltpu.VMEM((Z - 1, C2, R, w2), bf16),
            dma, dma((C2,)), dma((T * C,)), dma((T,)),
            dma((T - 1,)), dma((T - 1,)),
            dma((Z - 1, C)), dma((Z - 1, C)),
            dma((Y - 1, Z, C)), dma((Y - 1, Z, C)),
            dma((Y, Z, C)), dma((Y, Z, C)),
            dma((Y, C2)), dma((Y, C2)),
            dma((Y - 1, C2, 2)), dma((Y - 1, C2, 2)),
            dma((Z - 1, C2)), dma((Z - 1, C2)),
        ],
        compiler_params=pltpu.CompilerParams(
            collective_id=0, has_side_effects=True, vmem_limit_bytes=67000000
        ),
        name="feed_forward",
    )(
        counts, ranking, ranking, norm_gain, expand_bias, reduce_bias, flat, expand_weight, reduce_weight,
    )
    return result.reshape(images, patch_len, dl)


def solution(mesh):
    placed = (
        P(("groups", "dp"), None, "tensor"),
        P(("groups", "dp")),
        P(("groups", "dp"), None),
        P("tensor"),
        P(("dp", "tensor"), None),
        P(("dp", "tensor")),
        P(("dp", "tensor"), None),
        P("tensor"),
    )
    return jax.shard_map(
        functools.partial(body, mesh.shape["dp"], mesh.shape["tensor"]),
        mesh=mesh,
        in_specs=placed,
        out_specs=P(("groups", "dp"), None, "tensor"),
        check_vma=False,
    )
```

profile of v0, /device:TPU:0, one launch (start us, length us, event | category | flops | bytes accessed | tf_op | source)
XLA Modules:
  0.0 68.4 jit_solution(13421576317221783362)
XLA Ops:
  0.0 64.6 %feed_forward.1 = f32[512,1536]{1,0:T(8,128)} custom-call(s32[2]{0:T(128)} %counts.1, s32[2,256]{1,0:T(2,128)} %ranking_v.1, s32[2,256]{1,0:T(2,128)} %ranking_v.1, f32[1536]{0:T(1024)} %gain.1, bf16[1536]{0:T(1024)(128)(2,1)} %ebias.1, f32[1536]{0:T(1024)} %rbias.1, f32[512,1536]{1,0:T(8,128)} %bitcast.3, bf16[1536,6144]{1,0:T(8,128)(2,1)} %e_hbm.1, ...), custom_call_target="tpu_custom_call" | custom-call | tf_op jit(solution)/shard_map/feed_forward/pallas_call | solution.py:347
  64.6 3.8 %copy.10 = f32[2,256,1536]{2,1,0:T(8,128)} copy(f32[2,256,1536]{2,1,0:T(8,128)} %bitcast.2) | data formatting | bytes 6291456
where the time goes:
time: 68.6 us; the launch traced here: 68.4 us
  Pallas kernels  64.6 us (94%)
  local copies, waits for them, and re-layouts  3.76 us (5%)
    pallas_call x1, Pallas kernels, body(): pl.pallas_call(functools.partial(block_kernel, Z, T, C, C2), out_shape=ja...  64.6 us
    unnamed x1, local copies, waits for them, and re-layouts  3.76 us

commit v1 on v0

--- a/solution.py
+++ b/solution.py
@@ -12,9 +12,9 @@
 
 
 def block_kernel(
-    Z, T, C, C2, counts, ranking, ranking_v, gain, ebias, rbias, flat, e_hbm, r_hbm, out,
-    pt, rows, pick,    xg, wv, rv, pre, hid, bias, last, st, cs, cr, own, ys, yr, zs, zr,
-    psem, osem, wsem, rsem, st_s, st_r, za_s, za_r, ya_s, ya_r, ca_s, ca_r,
+    Z, T, C, C2, counts, ranking, ranking_v, gain, ebias, rbias, flat, e_hbm, r_hbm, pt,
+    rows, pick,    xg, wv, rv, pre, hid, bias, last, st, cs, cr, own, ys, yr, zs, zr,
+    psem, wsem, rsem, st_s, st_r, za_s, za_r, ya_s, ya_r, ca_s, ca_r,
     cr_s, cr_r, yr_s, yr_r, zr_s, zr_r,
 ):
     Y = T // 2
@@ -295,11 +295,7 @@
         spread = spread + jnp.dot(pick[...], middle, preferred_element_type=jnp.float32)
         spread = spread + jnp.dot(pick[...], top, preferred_element_type=jnp.float32)
         pt[:, cols] = pt[:, cols] + spread
-        save(p).start()
-
-    def save(p):
-        cols = columns(p)
-        return pltpu.make_async_copy(pt.at[:, cols], out.at[:, cols], osem.at[p])
+
 
     loop(0, C2, finish)
 
@@ -315,7 +311,6 @@
                 c_copy(u, j, p).wait_send()
 
     def drain(p):
-        save(p).wait()
         for u in range(Y):
             cr_copy(u, p).wait_send()
         for u in range(1, Y):
@@ -346,11 +341,10 @@
     smem = pl.BlockSpec(memory_space=pltpu.SMEM)
     result = pl.pallas_call(
         functools.partial(block_kernel, Z, T, C, C2),
-        out_shape=jax.ShapeDtypeStruct((N, dl), f32),
+        out_shape=pltpu.VMEM((N, dl), f32),
         in_specs=[smem] * 2 + [vmem] * 4 + [hbm] * 3,
-        out_specs=hbm,
+        out_specs=vmem,
         scratch_shapes=[
-            pltpu.VMEM((N, dl), f32),
             pltpu.VMEM((R, dl), f32),
             pltpu.VMEM((N, R), bf16),
             pltpu.VMEM((T, C, M, dlc), bf16),
@@ -368,7 +362,7 @@
             pltpu.VMEM((Y - 1, C2, M, w2), bf16),
             pltpu.VMEM((C2, M, w2), bf16),
             pltpu.VMEM((Z - 1, C2, R, w2), bf16),
-            dma, dma((C2,)), dma((T * C,)), dma((T,)),
+            dma, dma((T * C,)), dma((T,)),
             dma((T - 1,)), dma((T - 1,)),
             dma((Z - 1, C)), dma((Z - 1, C)),
             dma((Y - 1, Z, C)), dma((Y - 1, Z, C)),
@@ -378,7 +372,7 @@
             dma((Z - 1, C2)), dma((Z - 1, C2)),
         ],
         compiler_params=pltpu.CompilerParams(
-            collective_id=0, has_side_effects=True, vmem_limit_bytes=67000000
+            collective_id=0, has_side_effects=True, vmem_limit_bytes=63700000
         ),
         name="feed_forward",
     )(

time: 68.6 us -> 65.5 us (0.955)
  local copies, waits for them, and re-layouts: 3.76 us -> 1.67 us
  Pallas kernels: 64.6 us -> 63.7 us
    unnamed x1, local copies, waits for them, and re-layouts: 3.76 us -> 1.67 us
    pallas_call x1, Pallas kernels: 64.6 us -> 63.7 us  [body(): pl.pallas_call(functools.partial(block_kernel, Z, T, C, C2), out_shape=pl...]
where the time goes in v1:
time: 65.5 us; the launch traced here: 65.3 us
  Pallas kernels  63.7 us (97%)
  local copies, waits for them, and re-layouts  1.67 us (3%)
    pallas_call x1, Pallas kernels, body(): pl.pallas_call(functools.partial(block_kernel, Z, T, C, C2), out_shape=pl...  63.7 us
    unnamed x1, local copies, waits for them, and re-layouts  1.67 us

profile of v1, /device:TPU:0, one launch (start us, length us, event | category | flops | bytes accessed | tf_op | source)
XLA Modules:
  0.0 65.3 jit_solution(15334688507313427384)
XLA Ops:
  0.0 63.7 %feed_forward.1 = f32[512,1536]{1,0:T(8,128)S(1)} custom-call(s32[2]{0:T(128)} %counts.1, s32[2,256]{1,0:T(2,128)} %ranking_v.1, s32[2,256]{1,0:T(2,128)} %ranking_v.1, f32[1536]{0:T(1024)} %gain.1, bf16[1536]{0:T(1024)(128)(2,1)} %ebias.1, f32[1536]{0:T(1024)} %rbias.1, f32[512,1536]{1,0:T(8,128)} %bitcast.3, bf16[1536,6144]{1,0:T(8,128)(2,1)} %e_hbm.1, ...), custom_call_target="tpu_custom_call" | custom-call | tf_op jit(solution)/shard_map/feed_forward/pallas_call | solution.py:342
  63.7 1.7 %copy.10 = f32[2,256,1536]{2,1,0:T(8,128)} copy(f32[2,256,1536]{2,1,0:T(8,128)S(1)} %bitcast.2) | data formatting | bytes 6291456

commit v2 on v1

v2 whole, which is shorter than its diff:
```python
import functools

import jax
import jax.numpy as jnp
from jax import lax
from jax.experimental import pallas as pl
from jax.experimental.pallas import tpu as pltpu
from jax.sharding import PartitionSpec as P

CAP = 64
MESH = pl.DeviceIdType.MESH


def block_kernel(
    Z, T, C, G, C2, NB, counts, ranking, ranking_v, gain, ebias, rbias, flat, e_hbm, r_hbm, pt,
    rows, pick,    xg, wv, rv, pre, hid, last, st, cs, cr, own, ys, yr, zs, zr, zl, yf,
    psem, wsem, rsem, st_s, st_r, za_s, za_r, ya_s, ya_r, ca_s, ca_r,
    cr_s, cr_r, yr_s, yr_r, zr_s, zr_r, zl_r, yf_s, yf_r,
):
    Y = T // 2
    R, dl = rows.shape
    images, patch_len = ranking.shape
    N = images * patch_len
    hl, D = e_hbm.shape
    M, dlc, w2 = Z * R, dl // C, dl // C2
    nt = 256 if hl % 256 == 0 else hl
    z = lax.axis_index("dp")
    t = lax.axis_index("tensor")
    y, c = t // 2, t % 2
    z_next = lax.rem(z + 1, Z)
    t_next = lax.rem(y + 1, Y) * 2 + c
    t_part = y * 2 + 1 - c

    barrier = pltpu.get_barrier_semaphore()
    for k in range(1, Z):
        pl.semaphore_signal(barrier, inc=1, device_id={"dp": lax.rem(z + k, Z)}, device_id_type=MESH)
    for k in range(1, T):
        pl.semaphore_signal(barrier, inc=1, device_id={"tensor": lax.rem(t + k, T)}, device_id_type=MESH)

    def copy(src, dst, ss, rs, axis, index):
        return pltpu.make_async_remote_copy(
            src_ref=src, dst_ref=dst, send_sem=ss, recv_sem=rs,
            device_id={axis: index}, device_id_type=MESH,
        )

    def t_of(u, core):
        return lax.rem(y - u + Y, Y) * 2 + core

    def t_red(u, core):
        return lax.rem(y - 1 - u + 2 * Y, Y) * 2 + core

    def loop(low, high, body):
        lax.fori_loop(low, high, lambda p, a: (body(p), a)[1], 0)

    def expand_load(n):
        q = n // T
        k = n - q * T
        u = k // 2
        core = c + (k - 2 * u) * (1 - 2 * c)
        lanes = pl.ds(pl.multiple_of(t_of(u, core) * dl + q * G * dlc, 128), G * dlc)
        return pltpu.make_async_copy(e_hbm.at[:, lanes], wv.at[n], wsem.at[n])

    def reduce_load(i):
        u = i // 2
        block = t_red(u, c + (i - 2 * u) * (1 - 2 * c))
        lanes = pl.ds(pl.multiple_of(block * dl, 128), dl)
        return pltpu.make_async_copy(r_hbm.at[:, lanes], rv.at[i], rsem.at[i])

    patch_load = pltpu.make_async_copy(flat, pt, psem)
    patch_load.start()

    lane_w = images * R
    which = lax.broadcasted_iota(jnp.int32, (1, lane_w), 1)
    rank, owner = jnp.full((1, lane_w), -1, jnp.int32), jnp.full((1, lane_w), -1, jnp.int32)
    start = 0
    for i in range(images):
        k = which - i * R
        live = (k >= 0) & (k < counts[i])
        owner = jnp.where(live, start + k, owner)
        start = start + counts[i]
        known = jnp.concatenate([ranking_v[i : i + 1, :R]] * images, axis=1)
        rank = jnp.where(live, i * patch_len + known, rank)
    chosen = jnp.where(lax.broadcasted_iota(jnp.int32, (N, lane_w), 0) == rank, 1.0, 0.0)
    slot = jnp.where(lax.broadcasted_iota(jnp.int32, (R, lane_w), 0) == owner, 1.0, 0.0)
    pick[...] = lax.dot_general(
        chosen.astype(jnp.bfloat16), slot.astype(jnp.bfloat16), (((1,), (1,)), ((), ())),
        preferred_element_type=jnp.float32,
    ).astype(jnp.bfloat16)

    def take(j, carry):
        start, source = 0, 0
        for i in range(images):
            offset = j - start
            inside = (offset >= 0) & (offset < counts[i])
            here = i * patch_len + ranking[i, jnp.clip(offset, 0, patch_len - 1)]
            source = jnp.where(inside, here, source)
            start = start + counts[i]
        rows[pl.ds(j, 1), :] = pt[pl.ds(source, 1), :]
        return carry

    patch_load.wait()
    loop(0, C // G * T, lambda n: expand_load(n).start())
    loop(0, T, lambda i: reduce_load(i).start())
    lax.fori_loop(0, R, take, 0, unroll=8)

    pre[...] = jnp.broadcast_to(ebias[...].astype(jnp.float32)[None, :], pre.shape)
    x = rows[...]
    s1 = jnp.sum(x, axis=1, keepdims=True)
    s2 = jnp.sum(x * x, axis=1, keepdims=True)
    place = lax.broadcasted_iota(jnp.int32, (R, 2 * R), 1) - lax.broadcasted_iota(jnp.int32, (R, 2 * R), 0)
    packed = jnp.sum(jnp.where(place == 0, s1, jnp.where(place == R, s2, 0.0)), axis=0, keepdims=True)
    st[t] = jnp.broadcast_to(packed, st.shape[1:])
    pl.semaphore_wait(barrier, Z + T - 2)

    def stat_copy(k):
        return copy(st.at[t], st.at[t], st_s.at[k - 1], st_r.at[k - 1], "tensor", lax.rem(t + k, T))

    for k in range(1, T):
        stat_copy(k).start()
    for k in range(1, T):
        stat_copy(k).wait_recv()
    both = st[0, 0:1, :]
    for k in range(1, T):
        both = both + st[k, 0:1, :]
    total = [
        jnp.sum(jnp.where(place == k * R, both, 0.0), axis=1, keepdims=True) for k in range(2)
    ]
    gain_row = gain[...][None, :]
    mean = total[0] / D
    var = total[1] / D - mean * mean
    scale = lax.rsqrt(var + 1e-06)
    mine = pl.ds(pl.multiple_of(z * R, R), R)
    for p in range(C):
        cols = slice(p * dlc, (p + 1) * dlc)
        xg[t, p, mine, :] = ((rows[:, cols] - mean) * scale * gain_row[:, cols]).astype(jnp.bfloat16)

    def rows_of(tt, p, zb):
        return xg.at[tt, p, pl.ds(pl.multiple_of(zb * R, R), R), :]

    def inside(i):
        return (i >= 0) & (i < Z)

    def z_copy(way, d, p):
        step = 1 - 2 * way
        ref = rows_of(t, p, z - step * (d - 1))
        return copy(ref, ref, za_s.at[way, d - 1, p], za_r.at[way, d - 1, p], "dp", z + step)

    def z_sends(way, d):
        step = 1 - 2 * way
        return inside(z - step * (d - 1)) & inside(z + step)

    def z_wait(way, d, p):
        ref = rows_of(t, p, 0)
        copy(ref, ref, za_s.at[way, d - 1, p], za_r.at[way, d - 1, p], "dp", z_next).wait_recv()

    def y_copy(u, zb, p):
        ref = rows_of(t_of(u - 1, c), p, zb)
        return copy(ref, ref, ya_s.at[u - 1, zb, p], ya_r.at[u - 1, zb, p], "tensor", t_next)

    def c_copy(u, p):
        ref = xg.at[t_of(u, c), p]
        return copy(ref, ref, ca_s.at[u, p], ca_r.at[u, p], "tensor", t_part)

    def z_send(d, p):
        for way in range(2):
            @pl.when(z_sends(way, d))
            def _():
                z_copy(way, d, p).start()

    def z_arrive(d, p):
        for way in range(2):
            step = 1 - 2 * way
            zb = z - step * d

            @pl.when(inside(zb))
            def _():
                z_wait(way, d, p)
                if d < Z - 1:
                    @pl.when(inside(z + step))
                    def _():
                        z_copy(way, d + 1, p).start()

                if Y > 1:
                    y_copy(1, zb, p).start()

    def expand(n):
        q = n // T
        k = n - q * T
        u = k // 2
        tt = t_of(u, c + (k - 2 * u) * (1 - 2 * c))
        pltpu.make_async_copy(e_hbm.at[:, pl.ds(0, G * dlc)], wv.at[n], wsem.at[n]).wait()
        acc = pre[...]
        for g in range(G):
            acc += lax.dot_general(
                xg[tt, q * G + g], wv[n, :, g * dlc : (g + 1) * dlc], (((1,), (1,)), ((), ())),
                preferred_element_type=jnp.float32,
            )
        pre[...] = acc

    def own_sends(p):
        z_send(1, p)
        if Y > 1:
            y_copy(1, z, p).start()

    loop(0, C, own_sends)
    for d in range(1, Z - 1):
        loop(0, C, functools.partial(z_arrive, d))

    Q = C // G
    dots = [(r, q) for r in range(2) for q in range(Q)]
    for u in range(1, Y):
        for q in range(Q + 1):
            dots += [(2 * u, q)] * (q < Q) + [(2 * u + 1, q - 1)] * (q > 0)

    def look(table, i):
        found = table[0]
        for j in range(1, len(table)):
            found = jnp.where(i == j, table[j], found)
        return found

    def step(i):
        r = look([dot[0] for dot in dots], i)
        q = look([dot[1] for dot in dots], i)
        u = r // 2
        odd = r - 2 * u

        @pl.when(r == 0)
        def _():
            for g in range(G):
                if Z > 1:
                    z_arrive(Z - 1, q * G + g)
                c_copy(0, q * G + g).start()

        @pl.when(odd == 1)
        def _():
            for g in range(G):
                c_copy(u, q * G + g).wait_recv()

        @pl.when((odd == 0) & (r > 0))
        def _():
            for g in range(G):
                p = q * G + g
                for zb in range(Z):
                    y_copy(u, zb, p).wait_recv()
                    if Y > 2:
                        @pl.when(u < Y - 1)
                        def _():
                            y_copy(u + 1, zb, p).start()
                c_copy(u, p).start()

        expand(q * T + r)

    loop(0, T * Q, step)

    def activate(n):
        units = slice(None) if nt == hl else pl.ds(pl.multiple_of(n * nt, nt), nt)
        hid[:, units] = jax.nn.gelu(pre[:, units], approximate=True).astype(jnp.bfloat16)

    if nt == hl:
        activate(0)
    else:
        loop(0, hl // nt, activate)

    def cr_copy(i):
        return copy(cs.at[i], cr.at[i], cr_s.at[i], cr_r.at[i], "tensor", t_part)

    def half_of(h):
        return slice(h * M // 2, (h + 1) * M // 2)

    def yr_copy(u, p, h):
        half = half_of(h)
        return copy(
            ys.at[u - 1, p, half, :], yr.at[u - 1, p, half, :],
            yr_s.at[u - 1, p, h], yr_r.at[u - 1, p, h], "tensor", t_next,
        )

    def yf_copy(b):
        return copy(yf.at[0, b], yf.at[1, b], yf_s.at[b], yf_r.at[b], "tensor", t_next)

    def rows_at(i):
        return pl.ds(pl.multiple_of(i * R, R), R)

    def zr_copy(slot, way, k):
        step = 1 - 2 * way
        src = zs.at[slot, rows_at(z + step * k), :]
        if k <= 2:
            dst, sem, there = zr.at[slot, way, k - 1], zr_r.at[slot, way, k - 1], z + step * k
        else:
            dst, sem, there = zl.at[slot, way, k - 3], zl_r.at[slot, way, k - 3], z + step
        return copy(src, dst, zr_s.at[slot, way, k - 1], sem, "dp", there)

    def zr_wait(slot, way, k):
        src = zs.at[slot, rows_at(0), :]
        copy(src, zr.at[slot, way, k - 1], zr_s.at[slot, way, k - 1], zr_r.at[slot, way, k - 1], "dp", z_next).wait_recv()

    def zl_wait(slot, way, k):
        src = zs.at[slot, rows_at(0), :]
        copy(src, zl.at[slot, way, k - 2], zr_s.at[slot, way, k - 1], zl_r.at[slot, way, k - 2], "dp", z_next).wait_recv()

    def z_scatter(slot, h):
        for k in range(Z - 1, 0, -1):
            for way in range(2):
                step = 1 - 2 * way
                to = (z + step * k >= h * Z // 2) & (z + step * k < (h + 1) * Z // 2)
                if 2 <= k < Z - 1:
                    to = to & jnp.logical_not(inside(z - step))

                @pl.when(to)
                def _():
                    zr_copy(slot, way, k).start()

    def z_relay(slot, at):
        for k in range(Z - 2, 1, -1):
            for way in range(2):
                step = 1 - 2 * way

                @pl.when(inside(z - step) & inside(z + step * k))
                def _():
                    zl_wait(slot, way, k)
                    part = rows_at(z + step * k)
                    v = own[at, part, :] + zl[slot, way, k - 2].astype(jnp.float32)
                    zs[slot, part, :] = v.astype(jnp.bfloat16)
                    zr_copy(slot, way, k).start()

    def z_total(slot, at):
        for way in range(2):
            for k in range(1, min(Z - 1, 2) + 1):
                @pl.when(inside(z - (1 - 2 * way) * k))
                def _():
                    zr_wait(slot, way, k)
                    own[at, mine, :] += zr[slot, way, k - 1].astype(jnp.float32)

    def columns(p):
        return slice(None) if C2 == 1 else pl.ds(pl.multiple_of(p * w2, w2), w2)

    NA = C2 - NB
    first = [(0, p) for p in range(NA)]
    if NB:
        rest = [(u, NA + b) for u in range(Y) for b in range(NB)] + [(1, p) for p in range(NA)]
    else:
        rest = [(u, p) for u in range(1, Y) for p in range(NA)]
    order = []
    if NB:
        while first or rest:
            order += first[:1] + rest[:1]
            first, rest = first[1:], rest[1:]
    else:
        order = first + rest
    steps = len(order)

    def chunk(i):
        i = jnp.clip(i, 0, steps - 1)
        return look([o[0] for o in order], i), look([o[1] for o in order], i)

    def slot_of(u, p):
        return jnp.where(u == Y - 1, p, p + NB)

    def scattered(u, p):
        return (u == Y - 1) | (p >= NA)

    def produce(i):
        u, p = chunk(i)
        at = u * C2 + p

        def one(j):
            n = 2 * u + 1 - j
            to = jnp.where(j == 0, Y * C2, at)
            own[to] = jnp.dot(hid[...], rv[n, :, columns(p)], preferred_element_type=jnp.float32)

            @pl.when(j == 0)
            def _():
                cs[at] = own[Y * C2].astype(jnp.bfloat16)
                cr_copy(at).start()

        loop(0, 2, one)

    def combine(i):
        u, p = chunk(i)
        at = u * C2 + p
        cr_copy(at).wait_recv()
        ringed = (u > 0) & (p < NA)
        for h in range(2):
            half = half_of(h)
            own[at, half, :] += cr[at, half, :].astype(jnp.float32)

            @pl.when(ringed)
            def _():
                yr_copy(u, p, h).wait_recv()
                own[at, half, :] += yr[u - 1, p, half, :].astype(jnp.float32)

            @pl.when(scattered(u, p))
            def _():
                zs[slot_of(u, p), half, :] = own[at, half, :].astype(jnp.bfloat16)
                z_scatter(slot_of(u, p), h)

            @pl.when(jnp.logical_not(scattered(u, p)))
            def _():
                ys[u, p, half, :] = own[at, half, :].astype(jnp.bfloat16)
                yr_copy(u + 1, p, h).start()

    def relay(i):
        u, p = chunk(i)

        @pl.when(scattered(u, p))
        def _():
            z_relay(slot_of(u, p), u * C2 + p)

    def cross(b):
        at = NA + b
        z_total(C2 + b, at)
        yf[0, b] = own[at, mine, :].astype(jnp.bfloat16)
        yf_copy(b).start()

    def reduce(i):
        @pl.when(i == 0)
        def _():
            for j in range(T):
                reduce_load(j).wait()

        @pl.when(i < steps)
        def _():
            produce(i)

        @pl.when((i > 0) & (i <= steps))
        def _():
            combine(i - 1)

        if Z > 3:
            @pl.when(i > 3)
            def _():
                relay(i - 4)

        for b in range(NB):
            @pl.when(i == min(order.index((0, NA + b)) + 9, steps + 3))
            def _():
                cross(b)

    loop(0, steps + 4, reduce)

    last[...] = rbias[...][None, :]

    def sent(p):
        for d in range(1, Z):
            for way in range(2):
                @pl.when(z_sends(way, d))
                def _():
                    z_copy(way, d, p).wait_send()

        for u in range(1, Y):
            for zb in range(Z):
                y_copy(u, zb, p).wait_send()
        for u in range(Y):
            c_copy(u, p).wait_send()

    def drain(i):
        u, p = chunk(i)
        cr_copy(u * C2 + p).wait_send()

        @pl.when(jnp.logical_not(scattered(u, p)))
        def _():
            for h in range(2):
                yr_copy(u + 1, p, h).wait_send()

        @pl.when(scattered(u, p))
        def _():
            for k in range(1, Z):
                for way in range(2):
                    @pl.when(inside(z + (1 - 2 * way) * k))
                    def _():
                        zr_copy(slot_of(u, p), way, k).wait_send()

    def finish(i):
        @pl.when(i == C2 - 1)
        def _():
            for k in range(1, T):
                stat_copy(k).wait_send()
            loop(0, C, sent)
            loop(0, steps, drain)
            for b in range(NB):
                yf_copy(b).wait_send()

        p = lax.rem(i + NA, C2)
        at = (Y - 1) * C2 + p
        z_total(p, at)
        for b in range(NB):
            @pl.when(p == NA + b)
            def _():
                yf_copy(b).wait_recv()
                own[at, mine, :] += yf[1, b].astype(jnp.float32)

        cols = columns(p)
        add = own[at, mine, :] + last[:, cols]
        top = add.astype(jnp.bfloat16)
        rest = add - top.astype(jnp.float32)
        middle = rest.astype(jnp.bfloat16)
        low = (rest - middle.astype(jnp.float32)).astype(jnp.bfloat16)
        spread = jnp.dot(pick[...], low, preferred_element_type=jnp.float32)
        spread = spread + jnp.dot(pick[...], middle, preferred_element_type=jnp.float32)
        spread = spread + jnp.dot(pick[...], top, preferred_element_type=jnp.float32)
        pt[:, cols] = pt[:, cols] + spread

    loop(0, C2, finish)


def body(
    Z, T, patches, counts, ranking, norm_gain, expand_weight, expand_bias, reduce_weight, reduce_bias
):
    images, patch_len, dl = patches.shape
    hl, D = expand_weight.shape
    flat = patches.reshape(images * patch_len, dl)
    R, M, Y = CAP, Z * CAP, T // 2
    C = dl // 256 if dl % 256 == 0 else 1
    w2 = 256 if dl % 256 == 0 else dl
    C2 = dl // w2
    G = 2 if C % 2 == 0 else 1
    NB = 1 if Y == 2 and C2 > 4 else 0
    slots = C2 + NB
    dlc = dl // C
    vmem = pl.BlockSpec(memory_space=pltpu.VMEM)
    hbm = pl.BlockSpec(memory_space=pl.ANY)
    bf16, f32 = jnp.bfloat16, jnp.float32
    dma = pltpu.SemaphoreType.DMA
    N = images * patch_len
    smem = pl.BlockSpec(memory_space=pltpu.SMEM)
    result = pl.pallas_call(
        functools.partial(block_kernel, Z, T, C, G, C2, NB),
        out_shape=pltpu.VMEM((N, dl), f32),
        in_specs=[smem] * 2 + [vmem] * 4 + [hbm] * 3,
        out_specs=vmem,
        scratch_shapes=[
            pltpu.VMEM((R, dl), f32),
            pltpu.VMEM((N, R), bf16),
            pltpu.VMEM((T, C, M, dlc), bf16),
            pltpu.VMEM((T * C // G, hl, G * dlc), bf16),
            pltpu.VMEM((T, hl, dl), bf16),
            pltpu.VMEM((M, hl), f32),
            pltpu.VMEM((M, hl), bf16),
            pltpu.VMEM((1, dl), f32),
            pltpu.VMEM((T, 8, 2 * R), f32),
            pltpu.VMEM((Y * C2, M, w2), bf16),
            pltpu.VMEM((Y * C2, M, w2), bf16),
            pltpu.VMEM((Y * C2 + 1, M, w2), f32),
            pltpu.VMEM((Y - 1, C2, M, w2), bf16),
            pltpu.VMEM((Y - 1, C2, M, w2), bf16),
            pltpu.VMEM((slots, M, w2), bf16),
            pltpu.VMEM((slots, 2, 2, R, w2), bf16),
            pltpu.VMEM((slots, 2, max(Z - 3, 1), R, w2), bf16),
            pltpu.VMEM((2, max(NB, 1), R, w2), bf16),
            dma, dma((T * C // G,)), dma((T,)),
            dma((T - 1,)), dma((T - 1,)),
            dma((2, Z - 1, C)), dma((2, Z - 1, C)),
            dma((Y - 1, Z, C)), dma((Y - 1, Z, C)),
            dma((Y, C)), dma((Y, C)),
            dma((Y * C2,)), dma((Y * C2,)),
            dma((Y - 1, C2, 2)), dma((Y - 1, C2, 2)),
            dma((slots, 2, Z - 1)), dma((slots, 2, 2)), dma((slots, 2, max(Z - 3, 1))),
            dma((max(NB, 1),)), dma((max(NB, 1),)),
        ],
        compiler_params=pltpu.CompilerParams(
            collective_id=0, has_side_effects=True, vmem_limit_bytes=63700000
        ),
        name="feed_forward",
    )(
        counts, ranking, ranking, norm_gain, expand_bias, reduce_bias, flat, expand_weight, reduce_weight,
    )
    return result.reshape(images, patch_len, dl)


def solution(mesh):
    placed = (
        P(("groups", "dp"), None, "tensor"),
        P(("groups", "dp")),
        P(("groups", "dp"), None),
        P("tensor"),
        P(("dp", "tensor"), None),
        P(("dp", "tensor")),
        P(("dp", "tensor"), None),
        P("tensor"),
    )
    return jax.shard_map(
        functools.partial(body, mesh.shape["dp"], mesh.shape["tensor"]),
        mesh=mesh,
        in_specs=placed,
        out_specs=P(("groups", "dp"), None, "tensor"),
        check_vma=False,
    )
```

time: 65.5 us -> 60.3 us (0.921)
  Pallas kernels: 63.7 us -> 58.4 us
    pallas_call x1, Pallas kernels: 63.7 us -> 58.4 us  [body(): pl.pallas_call(functools.partial(block_kernel, Z, T, C, G, C2, NB), out_s...]
where the time goes in v2:
time: 60.3 us; the launch traced here: 60.1 us
  Pallas kernels  58.4 us (97%)
  local copies, waits for them, and re-layouts  1.67 us (3%)
    pallas_call x1, Pallas kernels, body(): pl.pallas_call(functools.partial(block_kernel, Z, T, C, G, C2, NB), out_s...  58.4 us
    unnamed x1, local copies, waits for them, and re-layouts  1.67 us

profile of v2, /device:TPU:0, one launch (start us, length us, event | category | flops | bytes accessed | tf_op | source)
XLA Modules:
  0.0 60.1 jit_solution(9418270817681764388)
XLA Ops:
  0.0 58.4 %feed_forward.1 = f32[512,1536]{1,0:T(8,128)S(1)} custom-call(s32[2]{0:T(128)} %counts.1, s32[2,256]{1,0:T(2,128)} %ranking_v.1, s32[2,256]{1,0:T(2,128)} %ranking_v.1, f32[1536]{0:T(1024)} %gain.1, bf16[1536]{0:T(1024)(128)(2,1)} %ebias.1, f32[1536]{0:T(1024)} %rbias.1, f32[512,1536]{1,0:T(8,128)} %bitcast.3, bf16[1536,6144]{1,0:T(8,128)(2,1)} %e_hbm.1, ...), custom_call_target="tpu_custom_call" | custom-call | tf_op jit(solution)/shard_map/feed_forward/pallas_call | solution.py:525
  58.4 1.7 %copy.10 = f32[2,256,1536]{2,1,0:T(8,128)} copy(f32[2,256,1536]{2,1,0:T(8,128)S(1)} %bitcast.2) | data formatting | bytes 6291456

commit v3 on v2

--- a/solution.py
+++ b/solution.py
@@ -8,6 +8,7 @@
 from jax.sharding import PartitionSpec as P
 
 CAP = 64
+LAST = 1
 MESH = pl.DeviceIdType.MESH
 
 
@@ -58,13 +59,13 @@
         u = k // 2
         core = c + (k - 2 * u) * (1 - 2 * c)
         lanes = pl.ds(pl.multiple_of(t_of(u, core) * dl + q * G * dlc, 128), G * dlc)
-        return pltpu.make_async_copy(e_hbm.at[:, lanes], wv.at[n], wsem.at[n])
+        return pltpu.make_async_copy(e_hbm.at[:, lanes], wv.at[n], wsem.at[q])
 
     def reduce_load(i):
         u = i // 2
         block = t_red(u, c + (i - 2 * u) * (1 - 2 * c))
         lanes = pl.ds(pl.multiple_of(block * dl, 128), dl)
-        return pltpu.make_async_copy(r_hbm.at[:, lanes], rv.at[i], rsem.at[i])
+        return pltpu.make_async_copy(r_hbm.at[:, lanes], rv.at[i], rsem)
 
     patch_load = pltpu.make_async_copy(flat, pt, psem)
     patch_load.start()
@@ -99,8 +100,6 @@
         return carry
 
     patch_load.wait()
-    loop(0, C // G * T, lambda n: expand_load(n).start())
-    loop(0, T, lambda i: reduce_load(i).start())
     lax.fori_loop(0, R, take, 0, unroll=8)
 
     pre[...] = jnp.broadcast_to(ebias[...].astype(jnp.float32)[None, :], pre.shape)
@@ -113,12 +112,15 @@
     pl.semaphore_wait(barrier, Z + T - 2)
 
     def stat_copy(k):
-        return copy(st.at[t], st.at[t], st_s.at[k - 1], st_r.at[k - 1], "tensor", lax.rem(t + k, T))
+        return copy(st.at[t], st.at[t], st_s, st_r, "tensor", lax.rem(t + k, T))
 
     for k in range(1, T):
         stat_copy(k).start()
-    for k in range(1, T):
-        stat_copy(k).wait_recv()
+    loop(0, C // G * T, lambda n: expand_load(n).start())
+    loop(0, T, lambda i: reduce_load(i).start())
+    others = st.at[0 : T - 1]
+    stats = copy(others, others, st_s, st_r, "tensor", t_part)
+    stats.wait_recv()
     both = st[0, 0:1, :]
     for k in range(1, T):
         both = both + st[k, 0:1, :]
@@ -143,7 +145,7 @@
     def z_copy(way, d, p):
         step = 1 - 2 * way
         ref = rows_of(t, p, z - step * (d - 1))
-        return copy(ref, ref, za_s.at[way, d - 1, p], za_r.at[way, d - 1, p], "dp", z + step)
+        return copy(ref, ref, za_s.at[way, d - 1], za_r.at[way, d - 1, p], "dp", z + step)
 
     def z_sends(way, d):
         step = 1 - 2 * way
@@ -151,15 +153,15 @@
 
     def z_wait(way, d, p):
         ref = rows_of(t, p, 0)
-        copy(ref, ref, za_s.at[way, d - 1, p], za_r.at[way, d - 1, p], "dp", z_next).wait_recv()
+        copy(ref, ref, za_s.at[way, d - 1], za_r.at[way, d - 1, p], "dp", z_next).wait_recv()
 
     def y_copy(u, zb, p):
         ref = rows_of(t_of(u - 1, c), p, zb)
-        return copy(ref, ref, ya_s.at[u - 1, zb, p], ya_r.at[u - 1, zb, p], "tensor", t_next)
+        return copy(ref, ref, ya_s.at[u - 1], ya_r.at[u - 1, p // G], "tensor", t_next)
 
     def c_copy(u, p):
         ref = xg.at[t_of(u, c), p]
-        return copy(ref, ref, ca_s.at[u, p], ca_r.at[u, p], "tensor", t_part)
+        return copy(ref, ref, ca_s.at[u], ca_r.at[u, p // G], "tensor", t_part)
 
     def z_send(d, p):
         for way in range(2):
@@ -188,7 +190,12 @@
         k = n - q * T
         u = k // 2
         tt = t_of(u, c + (k - 2 * u) * (1 - 2 * c))
-        pltpu.make_async_copy(e_hbm.at[:, pl.ds(0, G * dlc)], wv.at[n], wsem.at[n]).wait()
+
+        @pl.when(k == 0)
+        def _():
+            ref = wv.at[pl.ds(q * T, T)]
+            pltpu.make_async_copy(ref, ref, wsem.at[q]).wait()
+
         acc = pre[...]
         for g in range(G):
             acc += lax.dot_general(
@@ -233,18 +240,19 @@
 
         @pl.when(odd == 1)
         def _():
-            for g in range(G):
-                c_copy(u, q * G + g).wait_recv()
+            ref = xg.at[0, pl.ds(q * G, G)]
+            copy(ref, ref, ca_s.at[u], ca_r.at[u, q], "tensor", t_part).wait_recv()
 
         @pl.when((odd == 0) & (r > 0))
         def _():
+            ref = xg.at[0, pl.ds(q * G, G)]
+            copy(ref, ref, ya_s.at[u - 1], ya_r.at[u - 1, q], "tensor", t_next).wait_recv()
             for g in range(G):
                 p = q * G + g
-                for zb in range(Z):
-                    y_copy(u, zb, p).wait_recv()
-                    if Y > 2:
-                        @pl.when(u < Y - 1)
-                        def _():
+                if Y > 2:
+                    @pl.when(u < Y - 1)
+                    def _():
+                        for zb in range(Z):
                             y_copy(u + 1, zb, p).start()
                 c_copy(u, p).start()
 
@@ -262,7 +270,7 @@
         loop(0, hl // nt, activate)
 
     def cr_copy(i):
-        return copy(cs.at[i], cr.at[i], cr_s.at[i], cr_r.at[i], "tensor", t_part)
+        return copy(cs.at[i], cr.at[i], cr_s, cr_r.at[i], "tensor", t_part)
 
     def half_of(h):
         return slice(h * M // 2, (h + 1) * M // 2)
@@ -271,7 +279,7 @@
         half = half_of(h)
         return copy(
             ys.at[u - 1, p, half, :], yr.at[u - 1, p, half, :],
-            yr_s.at[u - 1, p, h], yr_r.at[u - 1, p, h], "tensor", t_next,
+            yr_s.at[u - 1], yr_r.at[u - 1, p, h], "tensor", t_next,
         )
 
     def yf_copy(b):
@@ -280,22 +288,21 @@
     def rows_at(i):
         return pl.ds(pl.multiple_of(i * R, R), R)
 
-    def zr_copy(slot, way, k):
+    def direct(slot):
+        return (slot >= NA - LAST) & (slot < NA)
+
+    def zr_copy(slot, way, k, whole=False):
         step = 1 - 2 * way
         src = zs.at[slot, rows_at(z + step * k), :]
-        if k <= 2:
-            dst, sem, there = zr.at[slot, way, k - 1], zr_r.at[slot, way, k - 1], z + step * k
+        if k <= 2 or whole:
+            dst, sem, there = zr.at[slot, way, k - 1], zr_r.at[slot, way], z + step * k
         else:
             dst, sem, there = zl.at[slot, way, k - 3], zl_r.at[slot, way, k - 3], z + step
-        return copy(src, dst, zr_s.at[slot, way, k - 1], sem, "dp", there)
-
-    def zr_wait(slot, way, k):
-        src = zs.at[slot, rows_at(0), :]
-        copy(src, zr.at[slot, way, k - 1], zr_s.at[slot, way, k - 1], zr_r.at[slot, way, k - 1], "dp", z_next).wait_recv()
+        return copy(src, dst, zr_s.at[way, k - 1], sem, "dp", there)
 
     def zl_wait(slot, way, k):
         src = zs.at[slot, rows_at(0), :]
-        copy(src, zl.at[slot, way, k - 2], zr_s.at[slot, way, k - 1], zl_r.at[slot, way, k - 2], "dp", z_next).wait_recv()
+        copy(src, zl.at[slot, way, k - 2], zr_s.at[way, k - 1], zl_r.at[slot, way, k - 2], "dp", z_next).wait_recv()
 
     def z_scatter(slot, h):
         for k in range(Z - 1, 0, -1):
@@ -303,7 +310,13 @@
                 step = 1 - 2 * way
                 to = (z + step * k >= h * Z // 2) & (z + step * k < (h + 1) * Z // 2)
                 if 2 <= k < Z - 1:
-                    to = to & jnp.logical_not(inside(z - step))
+                    to = to & (direct(slot) | jnp.logical_not(inside(z - step)))
+                if k > 2:
+                    @pl.when(to & direct(slot))
+                    def _():
+                        zr_copy(slot, way, k, True).start()
+
+                    to = to & jnp.logical_not(direct(slot))
 
                 @pl.when(to)
                 def _():
@@ -324,10 +337,17 @@
 
     def z_total(slot, at):
         for way in range(2):
-            for k in range(1, min(Z - 1, 2) + 1):
-                @pl.when(inside(z - (1 - 2 * way) * k))
+            count = z if way == 0 else Z - 1 - z
+            count = jnp.where(direct(slot), count, jnp.minimum(count, 2))
+            for k in range(1, Z):
+                @pl.when(count == k)
                 def _():
-                    zr_wait(slot, way, k)
+                    ref = zr.at[slot, way, 0:k]
+                    copy(ref, ref, zr_s.at[way, 0], zr_r.at[slot, way], "dp", z_next).wait_recv()
+
+            for k in range(1, Z):
+                @pl.when(count >= k)
+                def _():
                     own[at, mine, :] += zr[slot, way, k - 1].astype(jnp.float32)
 
     def columns(p):
@@ -401,7 +421,7 @@
     def relay(i):
         u, p = chunk(i)
 
-        @pl.when(scattered(u, p))
+        @pl.when(scattered(u, p) & jnp.logical_not(direct(slot_of(u, p))))
         def _():
             z_relay(slot_of(u, p), u * C2 + p)
 
@@ -414,70 +434,59 @@
     def reduce(i):
         @pl.when(i == 0)
         def _():
-            for j in range(T):
-                reduce_load(j).wait()
+            pltpu.make_async_copy(rv, rv, rsem).wait()
 
         @pl.when(i < steps)
         def _():
             produce(i)
 
+        if Z > 3:
+            @pl.when(i > 2)
+            def _():
+                relay(i - 3)
+
         @pl.when((i > 0) & (i <= steps))
         def _():
             combine(i - 1)
 
-        if Z > 3:
-            @pl.when(i > 3)
-            def _():
-                relay(i - 4)
-
         for b in range(NB):
-            @pl.when(i == min(order.index((0, NA + b)) + 9, steps + 3))
+            @pl.when(i == steps)
             def _():
                 cross(b)
 
-    loop(0, steps + 4, reduce)
+    loop(0, steps + 3, reduce)
 
     last[...] = rbias[...][None, :]
 
-    def sent(p):
-        for d in range(1, Z):
-            for way in range(2):
+    def drain():
+        stats.wait_send()
+        for way in range(2):
+            step = 1 - 2 * way
+            for d in range(1, Z):
                 @pl.when(z_sends(way, d))
                 def _():
-                    z_copy(way, d, p).wait_send()
-
+                    ref = xg.at[0, :, rows_at(0), :]
+                    copy(ref, ref, za_s.at[way, d - 1], za_r.at[way, 0, 0], "dp", z_next).wait_send()
+
+                @pl.when(inside(z + step * d))
+                def _():
+                    ref = zs.at[:, rows_at(0), :]
+                    copy(ref, ref, zr_s.at[way, d - 1], zr_r.at[0, way], "dp", z_next).wait_send()
+
+        for u in range(Y):
+            copy(xg.at[0], xg.at[0], ca_s.at[u], ca_r.at[u, 0], "tensor", t_part).wait_send()
+        copy(cs, cr, cr_s, cr_r.at[0], "tensor", t_part).wait_send()
         for u in range(1, Y):
-            for zb in range(Z):
-                y_copy(u, zb, p).wait_send()
-        for u in range(Y):
-            c_copy(u, p).wait_send()
-
-    def drain(i):
-        u, p = chunk(i)
-        cr_copy(u * C2 + p).wait_send()
-
-        @pl.when(jnp.logical_not(scattered(u, p)))
-        def _():
-            for h in range(2):
-                yr_copy(u + 1, p, h).wait_send()
-
-        @pl.when(scattered(u, p))
-        def _():
-            for k in range(1, Z):
-                for way in range(2):
-                    @pl.when(inside(z + (1 - 2 * way) * k))
-                    def _():
-                        zr_copy(slot_of(u, p), way, k).wait_send()
+            ref = ys.at[u - 1, 0:NA]
+            copy(xg.at[0], xg.at[0], ya_s.at[u - 1], ya_r.at[0, 0], "tensor", t_next).wait_send()
+            copy(ref, ref, yr_s.at[u - 1], yr_r.at[0, 0, 0], "tensor", t_next).wait_send()
+        for b in range(NB):
+            yf_copy(b).wait_send()
 
     def finish(i):
         @pl.when(i == C2 - 1)
         def _():
-            for k in range(1, T):
-                stat_copy(k).wait_send()
-            loop(0, C, sent)
-            loop(0, steps, drain)
-            for b in range(NB):
-                yf_copy(b).wait_send()
+            drain()
 
         p = lax.rem(i + NA, C2)
         at = (Y - 1) * C2 + p
@@ -543,17 +552,16 @@
             pltpu.VMEM((Y - 1, C2, M, w2), bf16),
             pltpu.VMEM((Y - 1, C2, M, w2), bf16),
             pltpu.VMEM((slots, M, w2), bf16),
-            pltpu.VMEM((slots, 2, 2, R, w2), bf16),
+            pltpu.VMEM((slots, 2, Z - 1, R, w2), bf16),
             pltpu.VMEM((slots, 2, max(Z - 3, 1), R, w2), bf16),
             pltpu.VMEM((2, max(NB, 1), R, w2), bf16),
-            dma, dma((T * C // G,)), dma((T,)),
-            dma((T - 1,)), dma((T - 1,)),
-            dma((2, Z - 1, C)), dma((2, Z - 1, C)),
-            dma((Y - 1, Z, C)), dma((Y - 1, Z, C)),
-            dma((Y, C)), dma((Y, C)),
-            dma((Y * C2,)), dma((Y * C2,)),
-            dma((Y - 1, C2, 2)), dma((Y - 1, C2, 2)),
-            dma((slots, 2, Z - 1)), dma((slots, 2, 2)), dma((slots, 2, max(Z - 3, 1))),
+            dma, dma((C // G,)), dma, dma, dma,
+            dma((2, Z - 1)), dma((2, Z - 1, C)),
+            dma((Y - 1,)), dma((Y - 1, C // G)),
+            dma((Y,)), dma((Y, C // G)),
+            dma, dma((Y * C2,)),
+            dma((Y - 1,)), dma((Y - 1, C2 - NB, 2)),
+            dma((2, Z - 1)), dma((slots, 2)), dma((slots, 2, max(Z - 3, 1))),
             dma((max(NB, 1),)), dma((max(NB, 1),)),
         ],
         compiler_params=pltpu.CompilerParams(

time: 60.3 us -> 57.6 us (0.955)
  Pallas kernels: 58.4 us -> 55.7 us
    pallas_call x1, Pallas kernels: 58.4 us -> 55.7 us  [body(): pl.pallas_call(functools.partial(block_kernel, Z, T, C, G, C2, NB), out_s...]
where the time goes in v3:
time: 57.6 us; the launch traced here: 57.4 us
  Pallas kernels  55.7 us (97%)
  local copies, waits for them, and re-layouts  1.67 us (3%)
    pallas_call x1, Pallas kernels, body(): pl.pallas_call(functools.partial(block_kernel, Z, T, C, G, C2, NB), out_s...  55.7 us
    unnamed x1, local copies, waits for them, and re-layouts  1.67 us

profile of v3, /device:TPU:0, one launch (start us, length us, event | category | flops | bytes accessed | tf_op | source)
XLA Modules:
  0.0 57.4 jit_solution(12231329175125570280)
XLA Ops:
  0.0 55.7 %feed_forward.1 = f32[512,1536]{1,0:T(8,128)S(1)} custom-call(s32[2]{0:T(128)} %counts.1, s32[2,256]{1,0:T(2,128)} %ranking_v.1, s32[2,256]{1,0:T(2,128)} %ranking_v.1, f32[1536]{0:T(1024)} %gain.1, bf16[1536]{0:T(1024)(128)(2,1)} %ebias.1, f32[1536]{0:T(1024)} %rbias.1, f32[512,1536]{1,0:T(8,128)} %bitcast.3, bf16[1536,6144]{1,0:T(8,128)(2,1)} %e_hbm.1, ...), custom_call_target="tpu_custom_call" | custom-call | tf_op jit(solution)/shard_map/feed_forward/pallas_call | solution.py:534
  55.7 1.7 %copy.10 = f32[2,256,1536]{2,1,0:T(8,128)} copy(f32[2,256,1536]{2,1,0:T(8,128)S(1)} %bitcast.2) | data formatting | bytes 6291456

commit v4 on v3

--- a/solution.py
+++ b/solution.py
@@ -88,19 +88,25 @@
         preferred_element_type=jnp.float32,
     ).astype(jnp.bfloat16)
 
-    def take(j, carry):
-        start, source = 0, 0
+    def source(j):
+        start, found = 0, 0
         for i in range(images):
             offset = j - start
-            inside = (offset >= 0) & (offset < counts[i])
+            inside_it = (offset >= 0) & (offset < counts[i])
             here = i * patch_len + ranking[i, jnp.clip(offset, 0, patch_len - 1)]
-            source = jnp.where(inside, here, source)
+            found = jnp.where(inside_it, here, found)
             start = start + counts[i]
-        rows[pl.ds(j, 1), :] = pt[pl.ds(source, 1), :]
-        return carry
+        return found
+
+    def take(g):
+        line = lax.broadcasted_iota(jnp.int32, (8, dl), 0)
+        eight = jnp.zeros((8, dl), jnp.float32)
+        for r in range(8):
+            eight = jnp.where(line == r, pt[pl.ds(source(g * 8 + r), 1), :], eight)
+        rows[pl.ds(pl.multiple_of(g * 8, 8), 8), :] = eight
 
     patch_load.wait()
-    lax.fori_loop(0, R, take, 0, unroll=8)
+    loop(0, R // 8, take)
 
     pre[...] = jnp.broadcast_to(ebias[...].astype(jnp.float32)[None, :], pre.shape)
     x = rows[...]

time: 57.6 us -> 57.6 us (level)
  no operation moved by 1% of the time
where the time goes in v4:
time: 57.6 us; the launch traced here: 57.4 us
  Pallas kernels  55.7 us (97%)
  local copies, waits for them, and re-layouts  1.67 us (3%)
    pallas_call x1, Pallas kernels, body(): pl.pallas_call(functools.partial(block_kernel, Z, T, C, G, C2, NB), out_s...  55.7 us
    unnamed x1, local copies, waits for them, and re-layouts  1.67 us

profile of v4, /device:TPU:0, one launch (start us, length us, event | category | flops | bytes accessed | tf_op | source)
XLA Modules:
  0.0 57.4 jit_solution(10904345661638657288)
XLA Ops:
  0.0 55.7 %feed_forward.1 = f32[512,1536]{1,0:T(8,128)S(1)} custom-call(s32[2]{0:T(128)} %counts.1, s32[2,256]{1,0:T(2,128)} %ranking_v.1, s32[2,256]{1,0:T(2,128)} %ranking_v.1, f32[1536]{0:T(1024)} %gain.1, bf16[1536]{0:T(1024)(128)(2,1)} %ebias.1, f32[1536]{0:T(1024)} %rbias.1, f32[512,1536]{1,0:T(8,128)} %bitcast.3, bf16[1536,6144]{1,0:T(8,128)(2,1)} %e_hbm.1, ...), custom_call_target="tpu_custom_call" | custom-call | tf_op jit(solution)/shard_map/feed_forward/pallas_call | solution.py:540
  55.7 1.7 %copy.10 = f32[2,256,1536]{2,1,0:T(8,128)} copy(f32[2,256,1536]{2,1,0:T(8,128)S(1)} %bitcast.2) | data formatting | bytes 6291456

commit v5 on v4

--- a/solution.py
+++ b/solution.py
@@ -191,23 +191,23 @@
                 if Y > 1:
                     y_copy(1, zb, p).start()
 
-    def expand(n):
-        q = n // T
-        k = n - q * T
-        u = k // 2
-        tt = t_of(u, c + (k - 2 * u) * (1 - 2 * c))
-
-        @pl.when(k == 0)
+    def expand(u, q):
+        ref = xg.at[0, pl.ds(q * G, G)]
+        copy(ref, ref, ca_s.at[u], ca_r.at[u, q], "tensor", t_part).wait_recv()
+
+        @pl.when(u == 0)
         def _():
             ref = wv.at[pl.ds(q * T, T)]
             pltpu.make_async_copy(ref, ref, wsem.at[q]).wait()
 
         acc = pre[...]
-        for g in range(G):
-            acc += lax.dot_general(
-                xg[tt, q * G + g], wv[n, :, g * dlc : (g + 1) * dlc], (((1,), (1,)), ((), ())),
-                preferred_element_type=jnp.float32,
-            )
+        for odd in range(2):
+            tt = t_of(u, c if odd == 0 else 1 - c)
+            for g in range(G):
+                acc += lax.dot_general(
+                    xg[tt, q * G + g], wv[q * T + 2 * u + odd, :, g * dlc : (g + 1) * dlc],
+                    (((1,), (1,)), ((), ())), preferred_element_type=jnp.float32,
+                )
         pre[...] = acc
 
     def own_sends(p):
@@ -220,51 +220,43 @@
         loop(0, C, functools.partial(z_arrive, d))
 
     Q = C // G
-    dots = [(r, q) for r in range(2) for q in range(Q)]
-    for u in range(1, Y):
-        for q in range(Q + 1):
-            dots += [(2 * u, q)] * (q < Q) + [(2 * u + 1, q - 1)] * (q > 0)
-
     def look(table, i):
         found = table[0]
         for j in range(1, len(table)):
             found = jnp.where(i == j, table[j], found)
         return found
 
-    def step(i):
-        r = look([dot[0] for dot in dots], i)
-        q = look([dot[1] for dot in dots], i)
-        u = r // 2
-        odd = r - 2 * u
-
-        @pl.when(r == 0)
+    def arrive(u, q):
+        @pl.when(u == 0)
         def _():
             for g in range(G):
                 if Z > 1:
                     z_arrive(Z - 1, q * G + g)
-                c_copy(0, q * G + g).start()
-
-        @pl.when(odd == 1)
-        def _():
-            ref = xg.at[0, pl.ds(q * G, G)]
-            copy(ref, ref, ca_s.at[u], ca_r.at[u, q], "tensor", t_part).wait_recv()
-
-        @pl.when((odd == 0) & (r > 0))
+
+        @pl.when(u > 0)
         def _():
             ref = xg.at[0, pl.ds(q * G, G)]
             copy(ref, ref, ya_s.at[u - 1], ya_r.at[u - 1, q], "tensor", t_next).wait_recv()
-            for g in range(G):
-                p = q * G + g
-                if Y > 2:
-                    @pl.when(u < Y - 1)
-                    def _():
+            if Y > 2:
+                @pl.when(u < Y - 1)
+                def _():
+                    for g in range(G):
                         for zb in range(Z):
-                            y_copy(u + 1, zb, p).start()
-                c_copy(u, p).start()
-
-        expand(q * T + r)
-
-    loop(0, T * Q, step)
+                            y_copy(u + 1, zb, q * G + g).start()
+
+        for g in range(G):
+            c_copy(u, q * G + g).start()
+
+    def step(i):
+        @pl.when(i < Y * Q)
+        def _():
+            arrive(i // Q, lax.rem(i, Q))
+
+        @pl.when(i > 0)
+        def _():
+            expand((i - 1) // Q, lax.rem(i - 1, Q))
+
+    loop(0, Y * Q + 1, step)
 
     def activate(n):
         units = slice(None) if nt == hl else pl.ds(pl.multiple_of(n * nt, nt), nt)
@@ -278,13 +270,14 @@
     def cr_copy(i):
         return copy(cs.at[i], cr.at[i], cr_s, cr_r.at[i], "tensor", t_part)
 
-    def half_of(h):
-        return slice(h * M // 2, (h + 1) * M // 2)
+    parts = [
+        look([sorted(range(Z), key=lambda b: -abs(b - a))[h] for a in range(Z)], z) for h in range(Z)
+    ]
 
     def yr_copy(u, p, h):
-        half = half_of(h)
+        part = rows_at(parts[h])
         return copy(
-            ys.at[u - 1, p, half, :], yr.at[u - 1, p, half, :],
+            ys.at[u - 1, p, part, :], yr.at[u - 1, p, part, :],
             yr_s.at[u - 1], yr_r.at[u - 1, p, h], "tensor", t_next,
         )
 
@@ -297,36 +290,37 @@
     def direct(slot):
         return (slot >= NA - LAST) & (slot < NA)
 
-    def zr_copy(slot, way, k, whole=False):
+    def zr_copy(slot, way, k):
+        there = z + (1 - 2 * way) * k
+        return copy(
+            zs.at[slot, rows_at(there), :], zr.at[slot, way, k - 1],
+            zr_s.at[way, k - 1], zr_r.at[slot, way], "dp", there,
+        )
+
+    def zl_copy(slot, way, k):
         step = 1 - 2 * way
-        src = zs.at[slot, rows_at(z + step * k), :]
-        if k <= 2 or whole:
-            dst, sem, there = zr.at[slot, way, k - 1], zr_r.at[slot, way], z + step * k
-        else:
-            dst, sem, there = zl.at[slot, way, k - 3], zl_r.at[slot, way, k - 3], z + step
-        return copy(src, dst, zr_s.at[way, k - 1], sem, "dp", there)
+        return copy(
+            zs.at[slot, rows_at(z + step * k), :], zl.at[slot, way, k - 3],
+            zr_s.at[way, k - 1], zl_r.at[slot, way, k - 3], "dp", z + step,
+        )
 
     def zl_wait(slot, way, k):
         src = zs.at[slot, rows_at(0), :]
         copy(src, zl.at[slot, way, k - 2], zr_s.at[way, k - 1], zl_r.at[slot, way, k - 2], "dp", z_next).wait_recv()
 
-    def z_scatter(slot, h):
-        for k in range(Z - 1, 0, -1):
-            for way in range(2):
-                step = 1 - 2 * way
-                to = (z + step * k >= h * Z // 2) & (z + step * k < (h + 1) * Z // 2)
-                if 2 <= k < Z - 1:
-                    to = to & (direct(slot) | jnp.logical_not(inside(z - step)))
-                if k > 2:
-                    @pl.when(to & direct(slot))
-                    def _():
-                        zr_copy(slot, way, k, True).start()
-
-                    to = to & jnp.logical_not(direct(slot))
-
-                @pl.when(to)
-                def _():
-                    zr_copy(slot, way, k).start()
+    def z_scatter(slot, zb):
+        way = jnp.where(zb < z, 1, 0)
+        k = jnp.where(zb < z, z - zb, zb - z)
+        last_one = jnp.logical_not(inside(z - (1 - 2 * way)))
+
+        @pl.when((k > 0) & (direct(slot) | (k == 1) | ((k == 2) & last_one)))
+        def _():
+            zr_copy(slot, way, k).start()
+
+        if Z > 3:
+            @pl.when((k > 2) & last_one & jnp.logical_not(direct(slot)))
+            def _():
+                zl_copy(slot, way, k).start()
 
     def z_relay(slot, at):
         for k in range(Z - 2, 1, -1):
@@ -339,7 +333,7 @@
                     part = rows_at(z + step * k)
                     v = own[at, part, :] + zl[slot, way, k - 2].astype(jnp.float32)
                     zs[slot, part, :] = v.astype(jnp.bfloat16)
-                    zr_copy(slot, way, k).start()
+                    (zr_copy if k == 2 else zl_copy)(slot, way, k).start()
 
     def z_total(slot, at):
         for way in range(2):
@@ -405,23 +399,28 @@
         at = u * C2 + p
         cr_copy(at).wait_recv()
         ringed = (u > 0) & (p < NA)
-        for h in range(2):
-            half = half_of(h)
-            own[at, half, :] += cr[at, half, :].astype(jnp.float32)
+        for h in range(Z):
+            if h == 3 and Z > 3:
+                @pl.when(i == steps - 1)
+                def _():
+                    relay(steps - 2)
+
+            part = rows_at(parts[h])
+            own[at, part, :] += cr[at, part, :].astype(jnp.float32)
 
             @pl.when(ringed)
             def _():
                 yr_copy(u, p, h).wait_recv()
-                own[at, half, :] += yr[u - 1, p, half, :].astype(jnp.float32)
+                own[at, part, :] += yr[u - 1, p, part, :].astype(jnp.float32)
 
             @pl.when(scattered(u, p))
             def _():
-                zs[slot_of(u, p), half, :] = own[at, half, :].astype(jnp.bfloat16)
-                z_scatter(slot_of(u, p), h)
+                zs[slot_of(u, p), part, :] = own[at, part, :].astype(jnp.bfloat16)
+                z_scatter(slot_of(u, p), parts[h])
 
             @pl.when(jnp.logical_not(scattered(u, p)))
             def _():
-                ys[u, p, half, :] = own[at, half, :].astype(jnp.bfloat16)
+                ys[u, p, part, :] = own[at, part, :].astype(jnp.bfloat16)
                 yr_copy(u + 1, p, h).start()
 
     def relay(i):
@@ -447,7 +446,7 @@
             produce(i)
 
         if Z > 3:
-            @pl.when(i > 2)
+            @pl.when((i > 2) & (i != steps + 1))
             def _():
                 relay(i - 3)
 
@@ -489,12 +488,15 @@
         for b in range(NB):
             yf_copy(b).wait_send()
 
+    back = max(NA - 2, 0)
+    turn = list(range(back)) + list(range(NA, C2)) + list(range(back, NA))
+
     def finish(i):
         @pl.when(i == C2 - 1)
         def _():
             drain()
 
-        p = lax.rem(i + NA, C2)
+        p = look(turn, i)
         at = (Y - 1) * C2 + p
         z_total(p, at)
         for b in range(NB):
@@ -566,7 +568,7 @@
             dma((Y - 1,)), dma((Y - 1, C // G)),
             dma((Y,)), dma((Y, C // G)),
             dma, dma((Y * C2,)),
-            dma((Y - 1,)), dma((Y - 1, C2 - NB, 2)),
+            dma((Y - 1,)), dma((Y - 1, C2 - NB, Z)),
             dma((2, Z - 1)), dma((slots, 2)), dma((slots, 2, max(Z - 3, 1))),
             dma((max(NB, 1),)), dma((max(NB, 1),)),
         ],

time: 57.6 us -> 57.6 us (level)
  no operation moved by 1% of the time
where the time goes in v5:
time: 57.6 us; the launch traced here: 57.4 us
  Pallas kernels  55.7 us (97%)
  local copies, waits for them, and re-layouts  1.67 us (3%)
    pallas_call x1, Pallas kernels, body(): pl.pallas_call(functools.partial(block_kernel, Z, T, C, G, C2, NB), out_s...  55.7 us
    unnamed x1, local copies, waits for them, and re-layouts  1.67 us

profile of v5, /device:TPU:0, one launch (start us, length us, event | category | flops | bytes accessed | tf_op | source)
XLA Modules:
  0.0 57.4 jit_solution(17744554943720707551)
XLA Ops:
  0.0 55.7 %feed_forward.1 = f32[512,1536]{1,0:T(8,128)S(1)} custom-call(s32[2]{0:T(128)} %counts.1, s32[2,256]{1,0:T(2,128)} %ranking_v.1, s32[2,256]{1,0:T(2,128)} %ranking_v.1, f32[1536]{0:T(1024)} %gain.1, bf16[1536]{0:T(1024)(128)(2,1)} %ebias.1, f32[1536]{0:T(1024)} %rbias.1, f32[512,1536]{1,0:T(8,128)} %bitcast.3, bf16[1536,6144]{1,0:T(8,128)(2,1)} %e_hbm.1, ...), custom_call_target="tpu_custom_call" | custom-call | tf_op jit(solution)/shard_map/feed_forward/pallas_call | solution.py:542
  55.7 1.7 %copy.10 = f32[2,256,1536]{2,1,0:T(8,128)} copy(f32[2,256,1536]{2,1,0:T(8,128)S(1)} %bitcast.2) | data formatting | bytes 6291456
